TPU v7x, 256 devices: a whole 4x4x8 slice. The times are simulated.
256 devices in a mesh: tx: 16 (over x_lo, z), ty: 8 (over y, core), gz: 2 (over x_hi).
Axes of the slice: x: 4 (x_hi: 2, x_lo: 2; x = x_hi * 2 + x_lo), y: 4, z: 8, core: 2. Of those that a mesh axis runs over, the one named last changes fastest.
Arguments:
- design: float32 [512, 2048, 256], P('tx', 'ty', 'gz'), may hold values from 0.05 to 0.95
- forward_edges: float32 [2, 12, 524288], P(None, None, ('tx', 'ty', 'gz')), may hold values from -6 to 6
- adjoint_edges: float32 [2, 12, 524288], P(None, None, ('tx', 'ty', 'gz')), may hold values from -6 to 6
- edge_basis: float32 [24, 12], replicated, may hold values from -1.75 to 1.75
- quad_weights: float32 [8], replicated, may hold values from 0.05 to 0.25
- slot_weights: bfloat16 [32768, 16, 128], P(('tx', 'ty', 'gz')), may hold values from 0.049804688 to 1
- slot_elements: int32 [32768, 16], P(('tx', 'ty', 'gz')), may hold values from 0 to 2047
- slot_blocks: int32 [32768, 16], P(('tx', 'ty', 'gz')), may hold values from 0 to 8191
- slot_counts: int32 [256, 128], P(('tx', 'ty', 'gz')), may hold values from 1 to 16, 1024 in all within a row
Outputs:
- projected: float32 [512, 2048, 256], P('tx', 'ty', 'gz')
- element_density: float32 [524288], P(('tx', 'ty', 'gz'))
Inputs may be any that keep to these rules, and one draw needn't show every extreme that they name: `slot_counts`: in every row of each partition the counts sum to 128 * 16 // 2 and the largest equals 16.
All inputs are finite; a program needn't handle non-finite values.
Results may differ from a plain program's by a relative error of at most 0.00055.
Values may be sent and summed in bfloat16 or wider, within the bound.
A program may use at most 128 MiB of HBM per device.

v0:
```python
import math

import jax
import jax.numpy as jnp
from jax import lax
from jax.sharding import PartitionSpec as P

RADIUS = 8
BLOCK_VOX = 128


def sent_together(arrays, axis, split_dim, concat_dim, along):
    columns = [a.reshape(*a.shape[:along], -1) for a in arrays]
    both = jnp.concatenate(columns, axis=along)
    out, at, gathered = (
        lax.all_to_all(both, axis, split_axis=split_dim, concat_axis=concat_dim, tiled=True),
        0,
        [],
    )
    for a, column in zip(arrays, columns):
        piece = out[..., at : at + column.shape[along]]
        gathered.append(piece.reshape(*piece.shape[:along], *a.shape[along:]))
        at += column.shape[along]
    return tuple(gathered)


def extended(block, sides, width, periodic):
    for axis, dim in sides:
        count = lax.axis_size(axis)
        forward = [(i, i + 1) for i in range(count - 1)]
        if periodic:
            forward.append((count - 1, 0))
        backward = [(target, source) for source, target in forward]
        low = lax.ppermute(
            lax.slice_in_dim(block, block.shape[dim] - width, None, axis=dim), axis, forward
        )
        high = lax.ppermute(lax.slice_in_dim(block, 0, width, axis=dim), axis, backward)
        block = jnp.concatenate([low, block, high], axis=dim)
    return block


def filter_kernel(radius):
    values = [float(radius + 1 - abs(offset)) for offset in range(-radius, radius + 1)]
    total = sum(values)
    return [value / total for value in values]


def along(padded, kernel, dimension, length):
    summed = kernel[0] * lax.slice_in_dim(padded, 0, length, axis=dimension)
    for offset in range(1, len(kernel)):
        summed = summed + kernel[offset] * lax.slice_in_dim(
            padded, offset, offset + length, axis=dimension
        )
    return summed


def project(filtered):
    sharp = 8.0
    middle = 0.5
    span_total = math.tanh(sharp * middle) + math.tanh(sharp * (1.0 - middle))
    return (math.tanh(sharp * middle) + jnp.tanh(sharp * (filtered - middle))) / span_total


def sensitivity(edge_basis, quad_weights, forward_edges, adjoint_edges):
    highest = lax.Precision.HIGHEST
    forward_field = jnp.einsum("qk,rke->rqe", edge_basis, forward_edges, precision=highest)
    adjoint_field = jnp.einsum("qk,rke->rqe", edge_basis, adjoint_edges, precision=highest)
    product = forward_field[0] * adjoint_field[0] - forward_field[1] * adjoint_field[1]
    points = quad_weights.shape[0]
    product = product.reshape(3, points, -1).sum(axis=0)
    return jnp.dot(quad_weights, product, precision=highest)


def body(
    design,
    forward_edges,
    adjoint_edges,
    edge_basis,
    quad_weights,
    slot_weights,
    slot_elements,
    slot_blocks,
    slot_counts,
):
    cells_x, cells_y, cells_z = design.shape
    tile_count, capacity = slot_elements.shape
    sensitivities = sensitivity(edge_basis, quad_weights, forward_edges, adjoint_edges)
    live_slots = jnp.arange(capacity, dtype=jnp.int32)[None, :] < slot_counts[0][:, None]
    slot_value = jnp.where(live_slots, sensitivities[slot_elements], jnp.float32(0.0)).astype(
        jnp.bfloat16
    )
    arrived = (
        *sent_together((slot_weights, slot_value), ("tx", "ty"), 0, 0, 2),
        lax.all_to_all(slot_blocks, ("tx", "ty"), split_axis=0, concat_axis=0, tiled=True),
    )
    arrived_weights = arrived[0].astype(jnp.float32)
    arrived_blocks = arrived[2]
    deposits = arrived_weights * arrived[1].astype(jnp.float32)[..., None]
    block_count = cells_x * cells_y * cells_z // BLOCK_VOX
    gradient_blocks = jnp.zeros((block_count, BLOCK_VOX), jnp.float32)
    gradient_blocks = gradient_blocks.at[arrived_blocks.reshape(-1)].add(
        deposits.reshape(-1, BLOCK_VOX)
    )
    gradient = gradient_blocks.reshape(cells_x, cells_y, cells_z)
    updated = jnp.clip(design - 0.5 * gradient, 0.0, 1.0)
    kernel = filter_kernel(RADIUS)
    positions = (
        lax.axis_index("gz") * cells_z + jnp.arange(cells_z + 2 * RADIUS, dtype=jnp.int32) - RADIUS
    )
    inside = ((positions >= 0) & (positions < lax.axis_size("gz") * cells_z)).astype(jnp.float32)
    normaliser = along(inside, kernel, 0, cells_z)
    padded = extended(updated.astype(jnp.bfloat16), (("tx", 0),), RADIUS, True).astype(
        updated.dtype
    )
    smoothed = along(padded, kernel, 0, cells_x)
    padded = extended(smoothed, (("ty", 1),), RADIUS, True)
    smoothed = along(padded, kernel, 1, cells_y)
    padded = extended(smoothed, (("gz", 2),), RADIUS, False)
    smoothed = along(padded, kernel, 2, cells_z)
    projected = project(smoothed / normaliser[None, None, :])
    projected_blocks = projected.reshape(block_count, BLOCK_VOX)
    picked = projected_blocks[arrived_blocks]
    local_ratios = jnp.sum(arrived_weights * picked, axis=-1) / jnp.sum(arrived_weights, axis=-1)
    ratios = lax.all_to_all(local_ratios, ("tx", "ty"), split_axis=0, concat_axis=0, tiled=True)
    element_density = jnp.zeros((forward_edges.shape[2],), jnp.float32)
    element_density = element_density.at[slot_elements.reshape(-1)].add(
        jnp.where(live_slots, ratios, jnp.float32(0.0)).reshape(-1)
    )
    return (projected, element_density)


def solution(mesh):
    in_specs = (
        P("tx", "ty", "gz"),
        P(None, None, ("tx", "ty", "gz")),
        P(None, None, ("tx", "ty", "gz")),
        P(),
        P(),
        P(("tx", "ty", "gz"), None, None),
        P(("tx", "ty", "gz"), None),
        P(("tx", "ty", "gz"), None),
        P(("tx", "ty", "gz"), None),
    )
    out_specs = (P("tx", "ty", "gz"), P(("tx", "ty", "gz")))
    return jax.shard_map(body, mesh=mesh, in_specs=in_specs, out_specs=out_specs, check_vma=False)
```

profile of v0, /device:TPU:1, one launch (start us, length us, event | category | flops | bytes accessed | tf_op | source)
XLA Modules:
  0.0 260.6 jit_solution(16023112619711644293)
XLA Ops:
  0.6 0.0 copy-start
  0.6 1.4 copy.97
  2.1 14.9 %all-to-all-start = ((s32[128,1,16]{2,1,0:T(1,128)}), s32[128,1,16]{2,1,0:T(1,128)S(1)}, u32[]{:S(2)}, u32[]{:S(2)}) async-start(s32[128,1,16]{2,1,0:T(1,128)} %bitcast), calls=%async_computation | async-start | bytes 131072 | tf_op jit(solution)/shard_map/all_to_all | solution.py:94
  16.9 0.7 compare_select_fusion.3
  17.6 0.1 copy.100
  17.7 0.1 reshape.187
  17.8 1.5 convolution_bitcast_fusion.1
  19.4 1.5 convolution_bitcast_fusion
  21.0 0.8 fusion.121
  21.8 11.6 %gather_fusion = bf16[2048]{0:T(1024)(128)(2,1)S(1)} fusion(f32[2048]{0:T(1024)S(1)} %bitcast.34, s32[2048]{0:T(1024)S(1)} %broadcast_clamp_fusion.1), kind=kCustom, calls=%fused_computation | custom fusion | bytes 16384 | tf_op jit(solution)/shard_map/gather | solution.py:89
  33.5 0.1 gather.9
  33.6 0.1 copy.101
  33.7 0.5 copy.102
  34.2 1.2 pad_maximum_fusion.4
  35.4 12.4 %all-to-all-start.1 = ((bf16[128,16,129]{2,1,0:T(8,128)(2,1)}), bf16[128,16,129]{2,1,0:T(8,128)(2,1)S(1)}, u32[]{:S(2)}, u32[]{:S(2)}) async-start(bf16[128,16,129]{2,1,0:T(8,128)(2,1)} %pad_maximum_fusion.4), calls=%async_computation.1 | async-start | bytes 2097152 | tf_op jit(solution)/shard_map/all_to_all | solution.py:16
  47.8 0.1 copy.109
  47.9 0.1 reshape.182
  48.0 0.5 broadcast.224
  48.5 0.8 reduce.6
  49.3 0.1 reshape.180
  49.4 30.0 %all-to-all-done.1 = bf16[128,16,129]{2,1,0:T(8,128)(2,1)S(1)} async-done(((bf16[128,16,129]{2,1,0:T(8,128)(2,1)}), bf16[128,16,129]{2,1,0:T(8,128)(2,1)S(1)}, u32[]{:S(2)}, u32[]{:S(2)}) %all-to-all-start.1) | async-done | bytes 528416 | tf_op jit(solution)/shard_map/all_to_all | solution.py:16
  79.4 0.1 slice.353
  79.5 0.5 copy.115
  80.0 0.1 copy.104
  80.1 0.3 convert_multiply_fusion.1
  80.4 13.7 %scatter_custom_fusion = f32[8192,128]{1,0:T(8,128)} fusion(s32[2048]{0:T(1024)S(1)} %bitcast.41, f32[2048,128]{1,0:T(8,128)S(1)} %bitcast.38, f32[]{:T(128)} %constant.23.clone.1), kind=kCustom, calls=%fused_computation.192 | custom fusion | flops 262144 | bytes 4194308 | tf_op jit(solution)/shard_map/scatter-add | solution.py:101
  94.1 2.6 %broadcast_multiply_fusion = f32[8192,128]{1,0:T(8,128)S(1)} fusion(f32[8192,128]{1,0:T(8,128)} %scatter_custom_fusion), kind=kLoop, calls=%fused_computation.191 | loop fusion | flops 1048576 | bytes 8388608 | tf_op jit(solution)/shard_map/mul | solution.py:105
  96.7 0.8 copy-done.2
  97.6 0.7 clamp_convert_fusion
  98.3 0.1 fusion.125
  98.4 0.5 collective-permute-start
  98.9 3.1 %collective-permute-start.1 = (bf16[8,256,128]{2,1,0:T(8,128)(2,1)S(1)}, bf16[8,256,128]{2,1,0:T(8,128)(2,1)S(1)}, u32[]{:S(2)}, u32[]{:S(2)}) collective-permute-start(bf16[8,256,128]{2,1,0:T(8,128)(2,1)S(1)} %get-tuple-element.11), channel_id=1, source_target_pairs={{16,0},{32,16},{48,32},{64,48},{80,64},{96,80},{112,96},{128,112},... | collective-permute-start | bytes 1572872 | tf_op jit(solution)/shard_map/ppermute | solution.py:37
  102.1 12.2 %collective-permute-done = bf16[8,256,128]{2,1,0:T(8,128)(2,1)S(1)} collective-permute-done((bf16[8,256,128]{2,1,0:T(8,128)(2,1)S(1)}, bf16[8,256,128]{2,1,0:T(8,128)(2,1)S(1)}, u32[]{:S(2)}, u32[]{:S(2)}) %collective-permute-start) | collective-permute-done | bytes 524320 | tf_op jit(solution)/shard_map/ppermute | solution.py:34
  114.3 0.5 maximum_convert_fusion
  114.8 7.5 %fusion.93 = f32[32,256,128]{2,1,0:T(8,128)S(1)} fusion(f32[48,256,128]{2,1,0:T(8,128)S(1)} %maximum_convert_fusion), kind=kLoop, calls=%fused_computation.154 | loop fusion | flops 34603008 | bytes 75497472 | tf_op jit(solution)/shard_map/add | solution.py:51
  122.3 0.0 collective-permute-start.2
  122.3 0.5 collective-permute-start.3
  122.8 0.1 multiply_add_fusion
  122.9 1.4 collective-permute-done.2
  124.3 2.8 %collective-permute-done.3 = f32[32,8,128]{2,1,0:T(8,128)S(1)} collective-permute-done((f32[32,8,128]{2,1,0:T(8,128)S(1)}, f32[32,8,128]{2,1,0:T(8,128)S(1)}, u32[]{:S(2)}, u32[]{:S(2)}) %collective-permute-start.3) | collective-permute-done | bytes 131104 | tf_op jit(solution)/shard_map/ppermute | solution.py:37
  127.0 9.4 %fusion.3 = f32[32,256,128]{2,1,0:T(8,128)S(1)} fusion(f32[32,8,128]{2,1,0:T(8,128)S(1)} %collective-permute-done.3, f32[32,8,128]{2,1,0:T(8,128)S(1)} %collective-permute-done.2, f32[32,256,128]{2,1,0:T(8,128)S(1)} %fusion.93), kind=kLoop, calls=%fused_computation.49 | loop fusion | flops 51380224 | bytes 8650752 | tf_op jit(solution)/shard_map/add | solution.py:51
  136.5 4.8 %fusion.123 = (f32[32,256,8]{2,1,0:T(8,128)}, f32[32,256,8]{2,1,0:T(8,128)}) fusion(f32[32,256,128]{2,1,0:T(8,128)S(1)} %fusion.3), kind=kLoop, calls=%fused_computation.226 | loop fusion | bytes 1048576 | tf_op jit(solution)/shard_map/slice | solution.py:35
  141.3 2.8 %copy.105 = f32[32,256,8]{1,2,0:T(8,128)S(1)} copy(f32[32,256,8]{2,1,0:T(8,128)} %get-tuple-element.6) | data formatting | bytes 524288 | tf_op jit(solution)/shard_map/slice | solution.py:35
  144.1 2.8 %copy.107 = f32[32,256,8]{1,2,0:T(8,128)S(1)} copy(f32[32,256,8]{2,1,0:T(8,128)} %get-tuple-element.7) | data formatting | bytes 524288 | tf_op jit(solution)/shard_map/slice | solution.py:37
  146.9 1.3 collective-permute-start.5
  148.2 5.7 %collective-permute-start.4 = (f32[32,256,8]{1,2,0:T(8,128)S(1)}, f32[32,256,8]{1,2,0:T(8,128)S(1)}, u32[]{:S(2)}, u32[]{:S(2)}) collective-permute-start(f32[32,256,8]{1,2,0:T(8,128)S(1)} %copy.105), channel_id=1, source_target_pairs={{0,1},{2,3},{4,5},{6,7},{8,9},{10,11},{12,13},{14,15},{16,17},{18,... | collective-permute-start | bytes 786440 | tf_op jit(solution)/shard_map/ppermute | solution.py:34
  153.9 0.1 reshape.195
  154.0 3.7 %collective-permute-done.4 = f32[32,256,8]{1,2,0:T(8,128)S(1)} collective-permute-done((f32[32,256,8]{1,2,0:T(8,128)S(1)}, f32[32,256,8]{1,2,0:T(8,128)S(1)}, u32[]{:S(2)}, u32[]{:S(2)}) %collective-permute-start.4) | collective-permute-done | bytes 262176 | tf_op jit(solution)/shard_map/ppermute | solution.py:34
  157.7 2.6 copy.106
  160.3 2.6 copy.108
  162.9 54.6 %add_multiply_fusion = f32[32,256,128]{2,1,0:T(8,128)} fusion(f32[32,256,8]{2,1,0:T(8,128)} %copy.108, f32[32,256,128]{2,1,0:T(8,128)} %copy-done.1, f32[32,256,8]{2,1,0:T(8,128)} %copy.106, f32[128]{0:T(128)S(1)} %multiply_add_fusion), kind=kLoop, calls=%fused_computation.186 | loop fusion | flops 56623104 | bytes 8913408 | tf_op jit(solution)/shard_map/div | solution.py:61
  217.5 7.7 %gather_fusion.1 = f32[2048,128]{1,0:T(8,128)S(1)} fusion(f32[8192,128]{1,0:T(8,128)} %bitcast.35, s32[2048]{0:T(1024)S(1)} %broadcast_clamp_fusion), kind=kCustom, calls=%fused_computation.1 | custom fusion | bytes 2105344 | tf_op jit(solution)/shard_map/gather | solution.py:122
  225.2 0.6 convert_reduce_fusion
  225.8 0.1 copy.114
  225.9 0.1 copy.113
  226.0 0.7 copy.112
  226.7 9.7 %all-to-all-start.2 = ((f32[128,1,16]{2,1,0:T(1,128)}), f32[128,1,16]{2,1,0:T(1,128)S(1)}, u32[]{:S(2)}, u32[]{:S(2)}) async-start(f32[128,1,16]{2,1,0:T(1,128)} %copy.112), calls=%async_computation.2 | async-start | bytes 131072 | tf_op jit(solution)/shard_map/all_to_all | solution.py:124
  236.4 0.1 iota_compare_fusion
  236.5 0.1 lt.83
  236.6 10.6 %all-to-all-done.2 = f32[128,1,16]{2,1,0:T(1,128)S(1)} async-done(((f32[128,1,16]{2,1,0:T(1,128)}), f32[128,1,16]{2,1,0:T(1,128)S(1)}, u32[]{:S(2)}, u32[]{:S(2)}) %all-to-all-start.2) | async-done | bytes 8224 | tf_op jit(solution)/shard_map/all_to_all | solution.py:124
  247.2 0.5 broadcast.225
  247.7 0.8 reduce.7
  248.5 0.1 all_to_all.22
  248.6 11.9 %scatter_custom_fusion.1 = f32[2048]{0:T(1024)} fusion(s32[2048]{0:T(1024)S(1)} %bitcast.40, f32[2048]{0:T(1024)S(1)} %broadcast_select_fusion, f32[]{:T(128)} %constant.23.clone.1), kind=kCustom, calls=%fused_computation.219 | custom fusion | flops 2048 | bytes 8196 | tf_op jit(solution)/shard_map/scatter-add | solution.py:126
  (25 shorter events, 0.2 us)
Async XLA Ops:
  0.6 17.2 %copy-start = (f32[24,12]{0,1:T(8,128)S(1)}, f32[24,12]{0,1:T(8,128)}, u32[]{:S(2)}) copy-start(f32[24,12]{0,1:T(8,128)} %param.12) | copy-start | bytes 3460
  2.1 33.3 %all-to-all-start = ((s32[128,1,16]{2,1,0:T(1,128)}), s32[128,1,16]{2,1,0:T(1,128)S(1)}, u32[]{:S(2)}, u32[]{:S(2)}) async-start(s32[128,1,16]{2,1,0:T(1,128)} %bitcast), calls=%async_computation | async-start | bytes 131072 | tf_op jit(solution)/shard_map/all_to_all | solution.py:94
  21.8 11.8 %copy-start.5 = (s32[1,128]{1,0:T(1,128)S(1)}, s32[1,128]{1,0:T(1,128)}, u32[]{:S(2)}) copy-start(s32[1,128]{1,0:T(1,128)} %param.17) | copy-start | bytes 1540
  21.8 12.3 %copy-start.3 = (bf16[128,16,128]{2,1,0:T(8,128)(2,1)S(1)}, bf16[128,16,128]{2,1,0:T(8,128)(2,1)}, u32[]{:S(2)}) copy-start(bf16[128,16,128]{2,1,0:T(8,128)(2,1)} %param.14) | copy-start | bytes 1572868
  33.5 14.3 %copy-start.4 = (s32[128,16]{0,1:T(8,128)S(1)}, s32[128,16]{0,1:T(8,128)}, u32[]{:S(2)}) copy-start(s32[128,16]{0,1:T(8,128)} %param.15) | copy-start | bytes 24580
  35.4 44.1 %all-to-all-start.1 = ((bf16[128,16,129]{2,1,0:T(8,128)(2,1)}), bf16[128,16,129]{2,1,0:T(8,128)(2,1)S(1)}, u32[]{:S(2)}, u32[]{:S(2)}) async-start(bf16[128,16,129]{2,1,0:T(8,128)(2,1)} %pad_maximum_fusion.4), calls=%async_computation.1 | async-start | bytes 2097152 | tf_op jit(solution)/shard_map/all_to_all | solution.py:16
  94.1 3.4 %copy-start.2 = (f32[32,256,128]{2,1,0:T(8,128)S(1)}, f32[32,256,128]{2,1,0:T(8,128)}, u32[]{:S(2)}) copy-start(f32[32,256,128]{2,1,0:T(8,128)} %param.9) | copy-start | bytes 12582916
  98.4 15.9 %collective-permute-start = (bf16[8,256,128]{2,1,0:T(8,128)(2,1)S(1)}, bf16[8,256,128]{2,1,0:T(8,128)(2,1)S(1)}, u32[]{:S(2)}, u32[]{:S(2)}) collective-permute-start(bf16[8,256,128]{2,1,0:T(8,128)(2,1)S(1)} %get-tuple-element.10), channel_id=1, source_target_pairs={{0,16},{16,32},{32,48},{48,64},{64,80},{80,96},{96,112},{112,128},... | collective-permute-start | bytes 1572872 | tf_op jit(solution)/shard_map/ppermute | solution.py:34
  98.9 15.4 %collective-permute-start.1 = (bf16[8,256,128]{2,1,0:T(8,128)(2,1)S(1)}, bf16[8,256,128]{2,1,0:T(8,128)(2,1)S(1)}, u32[]{:S(2)}, u32[]{:S(2)}) collective-permute-start(bf16[8,256,128]{2,1,0:T(8,128)(2,1)S(1)} %get-tuple-element.11), channel_id=1, source_target_pairs={{16,0},{32,16},{48,32},{64,48},{80,64},{96,80},{112,96},{128,112},... | collective-permute-start | bytes 1572872 | tf_op jit(solution)/shard_map/ppermute | solution.py:37
  122.3 2.0 collective-permute-start.2
  122.3 4.7 %collective-permute-start.3 = (f32[32,8,128]{2,1,0:T(8,128)S(1)}, f32[32,8,128]{2,1,0:T(8,128)S(1)}, u32[]{:S(2)}, u32[]{:S(2)}) collective-permute-start(f32[32,8,128]{2,1,0:T(8,128)S(1)} %get-tuple-element.9), channel_id=1, source_target_pairs={{2,0},{4,2},{6,4},{8,6},{10,8},{12,10},{14,12},{0,14},{3,1},{5,3},... | collective-permute-start | bytes 393224 | tf_op jit(solution)/shard_map/ppermute | solution.py:37
  136.5 4.8 %copy-start.1 = (f32[32,256,128]{2,1,0:T(8,128)}, f32[32,256,128]{2,1,0:T(8,128)S(1)}, u32[]{:S(2)}) copy-start(f32[32,256,128]{2,1,0:T(8,128)S(1)} %fusion.3) | copy-start | bytes 12582916
  146.9 13.4 %collective-permute-start.5 = (f32[32,256,8]{1,2,0:T(8,128)S(1)}, f32[32,256,8]{1,2,0:T(8,128)S(1)}, u32[]{:S(2)}, u32[]{:S(2)}) collective-permute-start(f32[32,256,8]{1,2,0:T(8,128)S(1)} %copy.107), channel_id=1, source_target_pairs={{1,0},{3,2},{5,4},{7,6},{9,8},{11,10},{13,12},{15,14},{17,16},{19,... | collective-permute-start | bytes 786440 | tf_op jit(solution)/shard_map/ppermute | solution.py:37
  148.2 9.5 %collective-permute-start.4 = (f32[32,256,8]{1,2,0:T(8,128)S(1)}, f32[32,256,8]{1,2,0:T(8,128)S(1)}, u32[]{:S(2)}, u32[]{:S(2)}) collective-permute-start(f32[32,256,8]{1,2,0:T(8,128)S(1)} %copy.105), channel_id=1, source_target_pairs={{0,1},{2,3},{4,5},{6,7},{8,9},{10,11},{12,13},{14,15},{16,17},{18,... | collective-permute-start | bytes 786440 | tf_op jit(solution)/shard_map/ppermute | solution.py:34
  226.7 20.5 %all-to-all-start.2 = ((f32[128,1,16]{2,1,0:T(1,128)}), f32[128,1,16]{2,1,0:T(1,128)S(1)}, u32[]{:S(2)}, u32[]{:S(2)}) async-start(f32[128,1,16]{2,1,0:T(1,128)} %copy.112), calls=%async_computation.2 | async-start | bytes 131072 | tf_op jit(solution)/shard_map/all_to_all | solution.py:124
where the time goes:
time: 261 us
  other arithmetic  106 us (41%)
  waiting for transfers between devices  60.6 us (23%)
  starting transfers between devices  48.2 us (18%)
  local copies, waits for them, and re-layouts  41.1 us (16%)
  matrix products  3.91 us (1%)
    div x1, other arithmetic, project(): (math.tanh(sharp * middle) + jnp.tanh(sharp * (filtered - middle))) / spa...  54.6 us
    all_to_all x1, waiting for transfers between devices, sent_together(): lax.all_to_all(both, axis, split_axis=split_dim, concat_axis=concat_dim,...  30 us
    ppermute x3, waiting for transfers between devices, extended(): lax.ppermute(lax.slice_in_dim(block, block.shape[dim] - width, None, axis...  17.2 us
    add x3, other arithmetic, along(): summed + kernel[offset] * lax.slice_in_dim(padded, offset, offset + lengt...  17 us
    all_to_all x1, starting transfers between devices, body(): lax.all_to_all(slot_blocks, ('tx', 'ty'), split_axis=0, concat_axis=0, ti...  14.9 us
    scatter-add x1, other arithmetic, body(): gradient_blocks.at[arrived_blocks.reshape(-1)]  13.7 us
    all_to_all x1, starting transfers between devices, sent_together(): lax.all_to_all(both, axis, split_axis=split_dim, concat_axis=concat_dim,...  12.4 us
    scatter-add x1, other arithmetic, body(): element_density.at[slot_elements.reshape(-1)]  11.9 us
  transfers between devices with their start and end apart: 9, of which 6 were waited for; matrix products, arithmetic and copies ran while one was open for 9% of the time, Pallas kernels for 0%

commit v1 on v0

v1 whole, which is shorter than its diff:
```python
import functools
import math

import jax
import jax.numpy as jnp
from jax import lax
from jax.experimental import pallas as pl
from jax.experimental.pallas import tpu as pltpu
from jax.sharding import PartitionSpec as P

MESH = pl.DeviceIdType.MESH
NTX, NTY = 16, 8
TILES = NTX * NTY
VX, VY, VZ = 32, 256, 128
CAP = 16
R = 8
GROUPS = 8
PER = TILES // GROUPS
F32, BF16, I32 = jnp.float32, jnp.bfloat16, jnp.int32
HIGHEST = lax.Precision.HIGHEST


def iota(shape, dim):
    return lax.broadcasted_iota(I32, shape, dim)


def cone(distance):
    return jnp.maximum(0, R + 1 - jnp.abs(distance))


def tile_device(tile):
    return (lax.div(tile, NTY), lax.rem(tile, NTY), lax.axis_index("gz"))


def repeated(block):
    return jnp.concatenate([block] * (128 // block.shape[1]), axis=1)


def wait_bytes(ref, sem):
    pltpu.make_async_copy(ref, ref, sem).wait()


def live_mask(counts):
    column = jnp.broadcast_to(counts.astype(F32), (TILES, TILES)).T
    slot = jnp.bitwise_and(iota((TILES, 128), 1), CAP - 1).astype(F32)
    return slot < column


def deposit_kernel(
    design_hbm,
    fe_ref,
    ae_ref,
    basis_ref,
    quad_ref,
    weights_ref,
    elements_ref,
    blocks_ref,
    counts_ref,
    y_out,
    rim_out,
    w_out,
    blk_out,
    design,
    acc,
    u_ref,
    z_ref,
    meta_s,
    meta_r,
    lanes_ref,
    zsend,
    zrecv,
    ysend,
    yrecv,
    xsend,
    dsem,
    wsend,
    wrecv,
    msend,
    mrecv,
    zss,
    zrs,
    yss,
    yrs,
    xss,
    xrs,
):
    tx, ty, gz = lax.axis_index("tx"), lax.axis_index("ty"), lax.axis_index("gz")
    me = tx * NTY + ty
    barrier = pltpu.get_barrier_semaphore()

    def greet(k, carry):
        pl.semaphore_signal(
            barrier, inc=1, device_id=tile_device(lax.rem(me + k, TILES)), device_id_type=MESH
        )
        return carry

    lax.fori_loop(1, TILES, greet, 0)
    pl.semaphore_signal(barrier, inc=1, device_id=(tx, ty, 1 - gz), device_id_type=MESH)
    load_design = pltpu.make_async_copy(design_hbm, design, dsem.at[0])
    load_design.start()

    basis = basis_ref[...]
    point = jnp.bitwise_and(iota(basis.shape, 0), 7)
    quad = jnp.zeros(basis.shape, F32)
    for q in range(8):
        quad = jnp.where(point == q, quad_ref[q], quad)
    pair = lax.dot_general(
        basis * quad, basis, (((0,), (0,)), ((), ())), precision=HIGHEST, preferred_element_type=F32
    )
    real = jnp.dot(pair, ae_ref[0], precision=HIGHEST, preferred_element_type=F32)
    imag = jnp.dot(pair, ae_ref[1], precision=HIGHEST, preferred_element_type=F32)
    sens = jnp.sum(fe_ref[0] * real - fe_ref[1] * imag, axis=0, keepdims=True)
    sens = sens.astype(BF16).astype(F32)

    element = repeated(elements_ref[...])
    high, low = jnp.right_shift(element, 7), jnp.bitwise_and(element, 127)
    value = jnp.zeros((TILES, 128), F32)
    for h in range(sens.shape[1] // 128):
        row = jnp.broadcast_to(sens[:, h * 128 : (h + 1) * 128], (TILES, 128))
        value = jnp.where(high == h, jnp.take_along_axis(row, low, axis=1), value)
    value = jnp.where(live_mask(counts_ref[...]), value, 0.0)
    lane = iota((TILES, 128), 1)
    offset = jnp.bitwise_and(iota((TILES, 128), 0) + (TILES - me), 7)
    message = jnp.where(
        jnp.bitwise_and(lane, 31) < CAP, value, repeated(blocks_ref[...]).astype(F32)
    )
    message = jnp.where(jnp.right_shift(lane, 5) == jnp.right_shift(offset, 1), message, 0.0)
    meta_s[:, 0, :] = message
    lanes_ref[...] = (
        (iota((16, 16, 256), 0) * 16 + iota((16, 16, 256), 1)).astype(F32).astype(BF16)
    )

    pl.semaphore_wait(barrier, TILES)

    def send_meta(k, carry):
        tile = lax.rem(me + k, TILES)
        pltpu.make_async_remote_copy(
            src_ref=meta_s.at[tile],
            dst_ref=meta_r.at[k],
            send_sem=msend.at[0],
            recv_sem=mrecv.at[0],
            device_id=tile_device(tile),
            device_id_type=MESH,
        ).start()
        return carry

    def send_weights(k, carry):
        tile = lax.rem(me + k, TILES)
        pltpu.make_async_remote_copy(
            src_ref=weights_ref.at[tile],
            dst_ref=w_out.at[k],
            send_sem=wsend.at[0],
            recv_sem=wrecv.at[lax.div(k, PER)],
            device_id=tile_device(tile),
            device_id_type=MESH,
        ).start()
        return carry

    lax.fori_loop(1, TILES, send_meta, 0)
    lax.fori_loop(1, TILES, send_weights, 0)
    w_out[0] = weights_ref[me]
    meta_r[0] = meta_s[me]
    wait_bytes(meta_r.at[pl.ds(1, TILES - 1)], mrecv.at[0])

    row_lane = jnp.bitwise_and(iota((1, 128), 1), 31) < CAP

    def slots(r):
        even = meta_r[8 * r] + meta_r[8 * r + 2] + meta_r[8 * r + 4] + meta_r[8 * r + 6]
        odd = meta_r[8 * r + 1] + meta_r[8 * r + 3] + meta_r[8 * r + 5] + meta_r[8 * r + 7]
        values = jnp.where(row_lane, even, pltpu.roll(odd, CAP, 1))
        targets = jnp.where(row_lane, pltpu.roll(even, 128 - CAP, 1), odd).astype(I32)
        return values, targets

    for g in range(GROUPS):
        va, ta = slots(2 * g)
        vb, tb = slots(2 * g + 1)
        blk_out[pl.ds(2 * g, 1), :] = ta
        blk_out[pl.ds(2 * g + 1, 1), :] = tb
        values = jnp.broadcast_to(jnp.concatenate([va, vb], axis=1), (16, 256)).astype(BF16)
        targets = jnp.concatenate([ta, tb], axis=1)
        plane = jnp.right_shift(targets, 8)
        within = jnp.bitwise_and(targets, 255).astype(F32)
        if g == 0:
            wait_bytes(w_out.at[pl.ds(1, PER - 1)], wrecv.at[0])
        else:
            wait_bytes(w_out.at[pl.ds(g * PER, PER)], wrecv.at[g])
        chunk = w_out[pl.ds(g * PER, PER)].reshape(PER * CAP, 128)

        def deposit(x, carry, g=g, chunk=chunk, plane=plane, within=within, values=values):
            here = jnp.broadcast_to(jnp.where(plane == x, within, -1.0), (16, 256)).astype(BF16)
            spread = jnp.where(lanes_ref[...] == here[None], values[None], jnp.zeros((), BF16))
            added = jnp.dot(spread.reshape(256, 256), chunk, preferred_element_type=F32)
            if g == 0:
                acc[x] = added
            else:
                acc[x] += added
            return carry

        lax.fori_loop(0, VX, deposit, 0, unroll=2)

    load_design.wait()

    def update(x, carry):
        moved = jnp.clip(design[x] - 0.5 * acc[x], 0.0, 1.0)
        u_ref[x] = (moved - 0.5).astype(BF16)
        return carry

    lax.fori_loop(0, VX, update, 0)

    rim_planes = list(range(R)) + list(range(VX - R, VX))
    inner_planes = list(range(R, VX - R))
    halves = (rim_planes, inner_planes)

    edge = jnp.where(gz == 0, VZ - R, 0)
    zi, zl = iota((128, 128), 0), iota((128, 128), 1)
    for h, planes in enumerate(halves):
        packed = jnp.zeros((VY, 128), F32)
        for j, x in enumerate(planes):
            pick = jnp.logical_and(
                jnp.right_shift(zl, 3) == j, zi == edge + jnp.bitwise_and(zl, 7)
            )
            pick = jnp.where(pick, 1.0, 0.0).astype(BF16)
            packed = packed + jnp.dot(u_ref[x], pick, preferred_element_type=F32)
        zsend[h] = packed.astype(BF16)
        pltpu.make_async_remote_copy(
            src_ref=zsend.at[h],
            dst_ref=zrecv.at[h],
            send_sem=zss.at[h],
            recv_sem=zrs.at[h],
            device_id=(tx, ty, 1 - gz),
            device_id_type=MESH,
        ).start()

    band_z = cone(zi - zl).astype(F32).astype(BF16)
    halo_at = jnp.where(gz == 0, VZ, -R) + jnp.bitwise_and(zi, 7)
    halo_z = cone(halo_at - zl).astype(F32)
    global_z = gz * VZ + iota((1, 128), 1)
    total = jnp.zeros((1, 128), I32)
    for m in range(-R, R + 1):
        at = global_z + m
        total = total + jnp.where(jnp.logical_and(at >= 0, at < 2 * VZ), R + 1 - abs(m), 0)
    scale_z = 1.0 / total.astype(F32)

    up, down = lax.rem(ty + 1, NTY), lax.rem(ty + NTY - 1, NTY)
    for h, planes in enumerate(halves):
        wait_bytes(zrecv.at[h], zrs.at[h])
        halo = zrecv[h]
        for j in range(0, 16, 2):
            pieces = []
            for i in range(2):
                mine = jnp.where(jnp.right_shift(zi, 3) == j + i, halo_z, 0.0).astype(BF16)
                both = jnp.concatenate([u_ref[planes[j + i]], halo], axis=1)
                kernel = jnp.concatenate([band_z, mine], axis=0)
                smooth = jnp.dot(both, kernel, preferred_element_type=F32) * scale_z
                z_ref[planes[j + i]] = smooth.astype(BF16)
                pieces.append(smooth)
            at = h * 8 + j // 2
            ysend[0, at] = jnp.concatenate([p[:R] for p in pieces], axis=0).astype(BF16)
            ysend[1, at] = jnp.concatenate([p[VY - R :] for p in pieces], axis=0).astype(BF16)
        for d, target in ((0, down), (1, up)):
            pltpu.make_async_remote_copy(
                src_ref=ysend.at[d, pl.ds(h * 8, 8)],
                dst_ref=yrecv.at[d, pl.ds(h * 8, 8)],
                send_sem=yss.at[2 * h + d],
                recv_sem=yrs.at[2 * h + d],
                device_id=(tx, target, gz),
                device_id_type=MESH,
            ).start()

    band_y = cone(iota((VY, VY), 0) - iota((VY, VY), 1)).astype(F32).astype(BF16)
    oi, ki = iota((32, 32), 0), iota((32, 32), 1)
    same = jnp.right_shift(oi, 3) == jnp.right_shift(ki, 3)
    o8, k8 = jnp.bitwise_and(oi, 7), jnp.bitwise_and(ki, 7)
    below = cone(o8 - (k8 - R))
    above = cone((R + k8) - o8)
    rim_y = jnp.where(same, jnp.where(oi < 16, below, above), 0).astype(F32).astype(BF16)
    scale = 1.0 / ((R + 1) * (R + 1))
    left, right = lax.rem(tx + NTX - 1, NTX), lax.rem(tx + 1, NTX)
    for h, planes in enumerate(halves):
        for d in range(2):
            half = yrecv.at[d, pl.ds(h * 8, 8)]
            wait_bytes(half, yrs.at[2 * h + d])
        for j in range(0, 16, 2):
            a, b = planes[j], planes[j + 1]
            both = jnp.concatenate([z_ref[a], z_ref[b]], axis=1)
            smooth = jnp.dot(band_y, both, preferred_element_type=F32) * scale
            at = h * 8 + j // 2
            rims = jnp.concatenate([yrecv[1, at], yrecv[0, at]], axis=0)
            extra = jnp.dot(rim_y, rims, preferred_element_type=F32) * scale
            for i, x in enumerate((a, b)):
                mine = smooth[:, 128 * i : 128 * (i + 1)]
                top = mine[:R] + extra[R * i : R * (i + 1)]
                end = mine[VY - R :] + extra[16 + R * i : 16 + R * (i + 1)]
                full = jnp.concatenate([top, mine[R : VY - R], end], axis=0)
                y_out[x] = full
                if h == 0:
                    xsend[j + i] = full.astype(BF16)
        if h == 0:
            for d, target in ((0, left), (1, right)):
                pltpu.make_async_remote_copy(
                    src_ref=xsend.at[pl.ds(d * R, R)],
                    dst_ref=rim_out.at[pl.ds((1 - d) * R, R)],
                    send_sem=xss.at[d],
                    recv_sem=xrs.at[d],
                    device_id=(target, ty, gz),
                    device_id_type=MESH,
                ).start()

    for d in range(2):
        wait_bytes(rim_out.at[pl.ds((1 - d) * R, R)], xrs.at[d])
        wait_bytes(xsend.at[pl.ds(d * R, R)], xss.at[d])
    for h in range(2):
        wait_bytes(zsend.at[h], zss.at[h])
        for d in range(2):
            wait_bytes(ysend.at[d, pl.ds(h * 8, 8)], yss.at[2 * h + d])
    wait_bytes(meta_s.at[pl.ds(1, TILES - 1)], msend.at[0])
    wait_bytes(w_out.at[pl.ds(1, TILES - 1)], wsend.at[0])


def project_kernel(blk_ref, y_ref, rim_ref, w_ref, out_hbm, ratio_out, proj, picked, sem):
    scale = 1.0 / ((R + 1) * (R + 1))
    top = math.tanh(4.0)
    rows = 32
    strips = VY // rows

    def copy_out(s):
        span = pl.ds(pl.multiple_of(s * rows, rows), rows)
        return pltpu.make_async_copy(proj.at[:, span, :], out_hbm.at[:, span, :], sem.at[0])

    def strip(s, carry):
        span = pl.ds(pl.multiple_of(s * rows, rows), rows)

        def at(i):
            if i < 0:
                return rim_ref[i + R, span, :].astype(F32)
            if i >= VX:
                return rim_ref[i - VX + R, span, :].astype(F32)
            return y_ref[i, span, :]

        total = (R + 1) * at(0)
        for m in range(1, R + 1):
            total = total + (R + 1 - m) * (at(m) + at(-m))
        slope = at(R + 1) - at(0)
        for m in range(1, R + 1):
            slope = slope + (at(m) - at(-m))
        for o in range(VX):
            proj[o, span, :] = 0.5 + (0.5 / top) * jnp.tanh((8.0 * scale) * total)
            if o < VX - 1:
                total = total + slope
                if o < VX - 2:
                    slope = slope + (at(o + R + 2) - 2.0 * at(o + 1) + at(o - R))
        copy_out(s).start()
        return carry

    lax.fori_loop(0, strips, strip, 0)

    flat = proj.reshape(VX * VY, VZ)

    def gather(i, carry):
        r = lax.div(i, 4)
        base = lax.rem(i, 4) * 32
        for j in range(32):
            row = blk_ref[r, base + j]
            picked[pl.ds(i * 32 + j, 1), :] = flat[pl.ds(row, 1), :]
        return carry

    lax.fori_loop(0, TILES * CAP // 32, gather, 0)

    ones = jnp.ones((8, 128), BF16)
    lanes = (((1,), (1,)), ((), ()))
    for r in range(TILES * CAP // 128):
        w = w_ref[pl.ds(r * 8, 8)].reshape(128, 128)
        product = w.astype(F32) * picked[pl.ds(r * 128, 128), :]
        high = product.astype(BF16)
        low = (product - high.astype(F32)).astype(BF16)
        over = lax.dot_general(ones, high, lanes, preferred_element_type=F32)
        over = over + lax.dot_general(ones, low, lanes, preferred_element_type=F32)
        under = lax.dot_general(ones, w, lanes, preferred_element_type=F32)
        ratio_out[r] = (over / under)[:1]

    wait_bytes(proj, sem.at[0])


def return_kernel(ratio_ref, elements_ref, counts_ref, out_ref, recv, ssem, rsem):
    tx, ty = lax.axis_index("tx"), lax.axis_index("ty")
    me = tx * NTY + ty
    barrier = pltpu.get_barrier_semaphore()

    def greet(k, carry):
        pl.semaphore_signal(
            barrier, inc=1, device_id=tile_device(lax.rem(me + k, TILES)), device_id_type=MESH
        )
        return carry

    lax.fori_loop(1, TILES, greet, 0)
    pl.semaphore_wait(barrier, TILES - 1)

    def send(k, carry):
        pltpu.make_async_remote_copy(
            src_ref=ratio_ref.at[lax.div(k, 8)],
            dst_ref=recv.at[me],
            send_sem=ssem.at[0],
            recv_sem=rsem.at[0],
            device_id=tile_device(lax.rem(me + TILES - k, TILES)),
            device_id_type=MESH,
        ).start()
        return carry

    lax.fori_loop(1, TILES, send, 0)
    recv[me] = ratio_ref[0]

    offset = jnp.bitwise_and(iota((TILES, 128), 0) + (TILES - me), 7)
    chosen = jnp.right_shift(iota((TILES, 128), 1), 4) == offset
    element = jnp.where(chosen, repeated(elements_ref[...]), 0)
    element = jnp.sum(element.reshape(TILES // 8, 8, 128), axis=1)
    live = jnp.logical_and(chosen, live_mask(counts_ref[...]))
    high_e, low_e = jnp.right_shift(element, 7), jnp.bitwise_and(element, 127)

    wait_bytes(recv.at[pl.ds(1, TILES - 1)], rsem.at[0])
    ratio = jnp.where(live, recv[:, 0, :], 0.0)
    ratio = jnp.sum(ratio.reshape(TILES // 8, 8, 128), axis=1)
    total = jnp.zeros((32, 128), F32)
    lanes = (((1,), (1,)), ((), ()))
    for r in range(16):
        value = ratio[r : r + 1]
        high = value.astype(BF16).astype(F32)
        spread = jnp.where(iota((16, 128), 0) == high_e[r : r + 1], 1.0, 0.0)
        left = jnp.concatenate([spread * high, spread * (value - high)], axis=0).astype(BF16)
        right = jnp.where(iota((128, 128), 0) == low_e[r : r + 1], 1.0, 0.0).astype(BF16)
        total = total + lax.dot_general(left, right, lanes, preferred_element_type=F32)
    out_ref[...] = total[:16] + total[16:]
    wait_bytes(recv.at[pl.ds(1, TILES - 1)], ssem.at[0])


VMEM = pl.BlockSpec(memory_space=pltpu.VMEM)
SMEM = pl.BlockSpec(memory_space=pltpu.SMEM)
ANY = pl.BlockSpec(memory_space=pl.ANY)
DMA = pltpu.SemaphoreType.DMA
LIMIT = 60 << 20


def body(
    design,
    forward_edges,
    adjoint_edges,
    edge_basis,
    quad_weights,
    slot_weights,
    slot_elements,
    slot_blocks,
    slot_counts,
):
    shape = jax.ShapeDtypeStruct
    smooth, rims, weights, blocks = pl.pallas_call(
        deposit_kernel,
        name="deposit_and_smooth",
        out_shape=(
            shape((VX, VY, VZ), F32),
            shape((2 * R, VY, VZ), BF16),
            shape((TILES, CAP, 128), BF16),
            shape((TILES * CAP // 128, 128), I32),
        ),
        in_specs=[ANY, VMEM, VMEM, VMEM, SMEM, VMEM, VMEM, VMEM, VMEM],
        out_specs=(VMEM, VMEM, VMEM, VMEM),
        scratch_shapes=[
            pltpu.VMEM((VX, VY, VZ), F32),
            pltpu.VMEM((VX, VY, VZ), F32),
            pltpu.VMEM((VX, VY, VZ), BF16),
            pltpu.VMEM((VX, VY, VZ), BF16),
            pltpu.VMEM((TILES, 1, 128), F32),
            pltpu.VMEM((TILES, 1, 128), F32),
            pltpu.VMEM((16, 16, 256), BF16),
            pltpu.VMEM((2, VY, 128), BF16),
            pltpu.VMEM((2, VY, 128), BF16),
            pltpu.VMEM((2, 16, 16, 128), BF16),
            pltpu.VMEM((2, 16, 16, 128), BF16),
            pltpu.VMEM((2 * R, VY, VZ), BF16),
            DMA((1,)),
            DMA((1,)),
            DMA((GROUPS,)),
            DMA((1,)),
            DMA((1,)),
            DMA((2,)),
            DMA((2,)),
            DMA((4,)),
            DMA((4,)),
            DMA((2,)),
            DMA((2,)),
        ],
        compiler_params=pltpu.CompilerParams(
            collective_id=1, has_side_effects=True, vmem_limit_bytes=LIMIT
        ),
    )(
        design,
        forward_edges,
        adjoint_edges,
        edge_basis,
        quad_weights,
        slot_weights,
        slot_elements,
        slot_blocks,
        slot_counts,
    )
    projected, ratios = pl.pallas_call(
        project_kernel,
        name="smooth_x_and_project",
        out_shape=(
            shape((VX, VY, VZ), F32),
            shape((TILES * CAP // 128, 1, 128), F32),
        ),
        in_specs=[SMEM, VMEM, VMEM, VMEM],
        out_specs=(ANY, VMEM),
        scratch_shapes=[
            pltpu.VMEM((VX, VY, VZ), F32),
            pltpu.VMEM((TILES * CAP, 128), F32),
            DMA((1,)),
        ],
        compiler_params=pltpu.CompilerParams(vmem_limit_bytes=LIMIT),
    )(blocks, smooth, rims, weights)
    density = pl.pallas_call(
        return_kernel,
        name="return_ratios",
        out_shape=shape((16, 128), F32),
        in_specs=[VMEM, VMEM, VMEM],
        out_specs=VMEM,
        scratch_shapes=[pltpu.VMEM((TILES, 1, 128), F32), DMA((1,)), DMA((1,))],
        compiler_params=pltpu.CompilerParams(
            collective_id=2, has_side_effects=True, vmem_limit_bytes=LIMIT
        ),
    )(ratios, slot_elements, slot_counts)
    return projected, density.reshape(-1)


def solution(mesh):
    in_specs = (
        P("tx", "ty", "gz"),
        P(None, None, ("tx", "ty", "gz")),
        P(None, None, ("tx", "ty", "gz")),
        P(),
        P(),
        P(("tx", "ty", "gz"), None, None),
        P(("tx", "ty", "gz"), None),
        P(("tx", "ty", "gz"), None),
        P(("tx", "ty", "gz"), None),
    )
    out_specs = (P("tx", "ty", "gz"), P(("tx", "ty", "gz")))
    return jax.shard_map(body, mesh=mesh, in_specs=in_specs, out_specs=out_specs, check_vma=False)
```

time: 261 us -> 113 us (0.43)
  other arithmetic: 106 us -> 0 us
  Pallas kernels: 0 us -> 103 us
  waiting for transfers between devices: 60.6 us -> 0 us
  starting transfers between devices: 48.2 us -> 0 us
  local copies, waits for them, and re-layouts: 41.1 us -> 9.01 us
  matrix products: 3.91 us -> 0 us
    pallas_call x0 -> x3, Pallas kernels: none -> 103 us  [the longest x1 76.8 us: body(): pl.pallas_call(deposit_kernel, name='deposit_and_smooth', out_shape=(shap...]
    div x2 -> x0, other arithmetic: 54.6 us -> none  [the longest x1 54.6 us: project(): (math.tanh(sharp * middle) + jnp.tanh(sharp * (filtered - middle))) / spa...]
    all_to_all x3 -> x0, waiting for transfers between devices: 40.6 us -> none  [the longest x1 30 us: sent_together(): lax.all_to_all(both, axis, split_axis=split_dim, concat_axis=concat_dim,...]
    all_to_all x3 -> x0, starting transfers between devices: 37 us -> none  [the longest x1 14.9 us: body(): lax.all_to_all(slot_blocks, ('tx', 'ty'), split_axis=0, concat_axis=0, ti...]
    scatter-add x2 -> x0, other arithmetic: 25.6 us -> none  [the longest x1 13.7 us: body(): gradient_blocks.at[arrived_blocks.reshape(-1)]]
    ppermute x6 -> x0, waiting for transfers between devices: 20 us -> none  [the longest x3 17.2 us: extended(): lax.ppermute(lax.slice_in_dim(block, block.shape[dim] - width, None, axis...]
    gather x4 -> x0, local copies, waits for them, and re-layouts: 19.4 us -> none  [the longest x3 11.8 us: body(): sensitivities[slot_elements]]
    add x3 -> x0, other arithmetic: 17 us -> none  [along(): summed + kernel[offset] * lax.slice_in_dim(padded, offset, offset + lengt...]
  transfers between devices with their start and end apart: 9 -> 0, of which waited for: 6 -> 0; matrix products, arithmetic and copies ran while one was open for 9% -> 0% of each run, Pallas kernels for 0% -> 0%
where the time goes in v1:
time: 113 us
  Pallas kernels  103 us (91%)
  local copies, waits for them, and re-layouts  9.01 us (8%)
    pallas_call x1, Pallas kernels, body(): pl.pallas_call(deposit_kernel, name='deposit_and_smooth', out_shape=(shap...  76.8 us
    pallas_call x1, Pallas kernels, body(): pl.pallas_call(return_kernel, name='return_ratios', out_shape=shape((16,...  16 us
    pallas_call x1, Pallas kernels, body(): pl.pallas_call(project_kernel, name='smooth_x_and_project', out_shape=(sh...  10.5 us
    unnamed x6, local copies, waits for them, and re-layouts  9.01 us

profile of v1, /device:TPU:1, one launch (start us, length us, event | category | flops | bytes accessed | tf_op | source)
XLA Modules:
  0.0 113.0 jit_solution(15406019861957420245)
XLA Ops:
  0.6 1.4 %copy.13.basis_ref = f32[24,12]{1,0:T(8,128)} copy(f32[24,12]{0,1:T(8,128)} %param.12) | data formatting | bytes 2304 | tf_op args[3]
  2.0 1.4 %copy.14.elements_ref = s32[128,16]{1,0:T(8,128)} copy(s32[128,16]{0,1:T(8,128)} %param.15) | data formatting | bytes 16384 | tf_op args[6]
  3.4 1.4 %copy.15.blocks_ref = s32[128,16]{1,0:T(8,128)} copy(s32[128,16]{0,1:T(8,128)} %param.16) | data formatting | bytes 16384 | tf_op args[7]
  4.8 1.7 %copy.11.fe_ref = f32[2,12,2048]{2,1,0:T(8,128)} copy(f32[2,12,2048]{2,0,1:T(2,128)} %param.10) | data formatting | bytes 393216 | tf_op args[1]
  6.6 1.8 %copy.12.ae_ref = f32[2,12,2048]{2,1,0:T(8,128)} copy(f32[2,12,2048]{2,0,1:T(2,128)} %param.11) | data formatting | bytes 393216 | tf_op args[2]
  8.3 76.8 %deposit_and_smooth.1 = (f32[32,256,128]{2,1,0:T(8,128)}, bf16[16,256,128]{2,1,0:T(8,128)(2,1)}, bf16[128,16,128]{2,1,0:T(8,128)(2,1)}, s32[16,128]{1,0:T(8,128)}) custom-call(f32[32,256,128]{2,1,0:T(8,128)} %design_hbm.1, f32[2,12,2048]{2,1,0:T(8,128)} %copy.11.fe_ref, f32[2,12,2048]{2,1,0:T(8,128)} %copy.12.ae_ref, f32[24,12]{1,0:T(8,128)} %copy.13.basis_ref, ...), custom_call_target="tpu_custom_call" | custom-call | tf_op jit(solution)/shard_map/deposit_and_smooth/pallas_call | solution.py:454
  85.1 10.5 %smooth_x_and_project.1 = (f32[32,256,128]{2,1,0:T(8,128)}, f32[16,1,128]{2,1,0:T(1,128)}) custom-call(s32[16,128]{1,0:T(8,128)} %get-tuple-element.8.blk_ref, f32[32,256,128]{2,1,0:T(8,128)} %get-tuple-element.9.y_ref, bf16[16,256,128]{2,1,0:T(8,128)(2,1)} %get-tuple-element.10.rim_ref, bf16[128,16,128]{2,1,0:T(8,128)(2,1)} %get-tuple-element.11.w_ref), custom_call_target="tpu_custom_call" | custom-call | tf_op jit(solution)/shard_map/smooth_x_and_project/pallas_call | solution.py:504
  95.6 16.0 %return_ratios.1 = f32[16,128]{1,0:T(8,128)} custom-call(f32[16,1,128]{2,1,0:T(1,128)} %get-tuple-element.13.ratio_ref, s32[128,16]{1,0:T(8,128)} %copy.14.elements_ref, s32[1,128]{1,0:T(1,128)} %counts_ref.3), custom_call_target="tpu_custom_call" | custom-call | tf_op jit(solution)/shard_map/return_ratios/pallas_call | solution.py:520
  111.7 1.3 %copy.18 = f32[2048]{0:T(1024)} copy(f32[2048]{0:T(1024)} %bitcast.1) | data formatting | bytes 16384

commit v2 on v0

v2 whole, which is shorter than its diff:
```python
import math

import jax
import jax.numpy as jnp
from jax import lax
from jax.experimental import pallas as pl
from jax.experimental.pallas import tpu as pltpu
from jax.sharding import PartitionSpec as P

MESH = pl.DeviceIdType.MESH
NTX, NTY = 16, 8
TILES = NTX * NTY
VX, VY, VZ = 32, 256, 128
CAP = 16
R = 8
PER = 16
PIECES = 8
BATCHES = ((0, 4), (4, 2), (6, 2))
F32, BF16, I32 = jnp.float32, jnp.bfloat16, jnp.int32
HIGHEST = lax.Precision.HIGHEST


def iota(shape, dim):
    return lax.broadcasted_iota(I32, shape, dim)


def cone(distance):
    return jnp.maximum(0, R + 1 - jnp.abs(distance))


def tile_device(tile):
    return (lax.div(tile, NTY), lax.rem(tile, NTY), lax.axis_index("gz"))


def wait_bytes(ref, sem):
    pltpu.make_async_copy(ref, ref, sem).wait()


def live_mask(counts):
    return iota((CAP, TILES), 0) < counts


def step_kernel(
    design_hbm,
    fe_ref,
    ae_ref,
    basis_ref,
    quad_ref,
    weights_ref,
    elements_ref,
    blocks_ref,
    counts_ref,
    out_hbm,
    density_ref,
    design,
    acc,
    u_ref,
    z_ref,
    zx_ref,
    xrecv,
    y_ref,
    rim_ref,
    proj,
    picked,
    w_recv,
    meta_s,
    meta_r,
    lanes_ref,
    spread_ref,
    column_ref,
    blk_v,
    blk_s,
    ratios,
    returned,
    ysend,
    yrecv,
    yxrecv,
    packs,
    high_ref,
    low_ref,
    zsend,
    zrecv,
    zxrecv,
    esend,
    erecv,
    dsem,
    wsend,
    wrecv,
    msend,
    mrecv,
    hsend,
    hrecv,
    osem,
    bsem,
    rsend,
    rrecv,
):
    tx, ty, gz = lax.axis_index("tx"), lax.axis_index("ty"), lax.axis_index("gz")
    me = tx * NTY + ty
    barrier = pltpu.get_barrier_semaphore()

    def neighbour(dx, dy, dz):
        return (
            lax.rem(tx + (NTX + dx), NTX),
            lax.rem(ty + (NTY + dy), NTY),
            1 - gz if dz else gz,
        )

    def greet(k, carry):
        pl.semaphore_signal(
            barrier, inc=1, device_id=tile_device(lax.rem(me + k, TILES)), device_id_type=MESH
        )
        return carry

    lax.fori_loop(1, TILES, greet, 0)
    for dx in (-1, 0, 1):
        for dy in (-1, 0, 1):
            pl.semaphore_signal(
                barrier, inc=1, device_id=neighbour(dx, dy, 1), device_id_type=MESH
            )
    load_design = pltpu.make_async_copy(design_hbm, design, dsem.at[0])
    load_design.start()

    basis = basis_ref[...]
    point = jnp.bitwise_and(iota(basis.shape, 1), 7)
    quad = jnp.zeros(basis.shape, F32)
    for q in range(8):
        quad = jnp.where(point == q, quad_ref[q], quad)
    pair = lax.dot_general(
        basis * quad, basis, (((1,), (1,)), ((), ())), precision=HIGHEST, preferred_element_type=F32
    )
    real = jnp.dot(pair, ae_ref[:, 0, :], precision=HIGHEST, preferred_element_type=F32)
    imag = jnp.dot(pair, ae_ref[:, 1, :], precision=HIGHEST, preferred_element_type=F32)
    sens = jnp.sum(fe_ref[:, 0, :] * real - fe_ref[:, 1, :] * imag, axis=0, keepdims=True)
    sens = sens.astype(BF16).astype(F32)

    element = elements_ref[...]
    high, low = jnp.right_shift(element, 7), jnp.bitwise_and(element, 127)
    value = jnp.zeros((CAP, TILES), F32)
    for h in range(sens.shape[1] // 128):
        row = jnp.broadcast_to(sens[:, h * 128 : (h + 1) * 128], (CAP, TILES))
        value = jnp.where(high == h, jnp.take_along_axis(row, low, axis=1), value)
    value = jnp.where(live_mask(counts_ref[...]), value, 0.0)
    message = jnp.concatenate([value, blocks_ref[...].astype(F32)] * 4, axis=0)
    offset = jnp.bitwise_and(iota((128, TILES), 1) + (TILES - me), 7)
    chosen = jnp.right_shift(iota((128, TILES), 0), 5) == jnp.right_shift(offset, 1)
    meta_s[:, 0, :] = jnp.where(chosen, message, 0.0).T
    packs[...] = jnp.zeros(packs.shape, F32)
    for r in range(CAP):
        high_ref[:, 128 * r : 128 * (r + 1)] = jnp.where(
            iota((16, 128), 0) == high[r : r + 1], 1.0, 0.0
        )
        low_ref[:, 128 * r : 128 * (r + 1)] = jnp.where(
            iota((128, 128), 0) == low[r : r + 1], 1.0, 0.0
        ).astype(BF16)
    lanes_ref[...] = (
        (iota((16, 16, 256), 0) * 16 + iota((16, 16, 256), 1)).astype(F32).astype(BF16)
    )

    pl.semaphore_wait(barrier, TILES - 1 + 9)

    def sender(group):
        def send(k, carry):
            tile = lax.rem(me + k, TILES)
            pltpu.make_async_remote_copy(
                src_ref=meta_s.at[tile],
                dst_ref=meta_r.at[k],
                send_sem=msend.at[0],
                recv_sem=mrecv.at[group],
                device_id=tile_device(tile),
                device_id_type=MESH,
            ).start()
            pltpu.make_async_remote_copy(
                src_ref=weights_ref.at[tile],
                dst_ref=w_recv.at[k],
                send_sem=wsend.at[0],
                recv_sem=wrecv.at[group],
                device_id=tile_device(tile),
                device_id_type=MESH,
            ).start()
            return carry

        return send

    for group, (chunk, count) in enumerate(BATCHES):
        lax.fori_loop(max(1, chunk * PER), (chunk + count) * PER, sender(group), 0)
    w_recv[0] = weights_ref[me]
    meta_r[0] = meta_s[me]

    row_lane = jnp.bitwise_and(iota((1, 128), 1), 31) < CAP

    def slots(r):
        even = meta_r[8 * r] + meta_r[8 * r + 2] + meta_r[8 * r + 4] + meta_r[8 * r + 6]
        odd = meta_r[8 * r + 1] + meta_r[8 * r + 3] + meta_r[8 * r + 5] + meta_r[8 * r + 7]
        values = jnp.where(row_lane, even, pltpu.roll(odd, CAP, 1))
        targets = jnp.where(row_lane, pltpu.roll(even, 128 - CAP, 1), odd).astype(I32)
        blk_v[pl.ds(r, 1), :] = targets
        return values, targets

    def prepare(c):
        va, ta = slots(2 * c)
        vb, tb = slots(2 * c + 1)
        values = jnp.broadcast_to(jnp.concatenate([va, vb], axis=1), (16, 256)).astype(BF16)
        targets = jnp.concatenate([ta, tb], axis=1)
        within = jnp.bitwise_and(targets, 255).astype(F32)
        within = jnp.broadcast_to(within, (16, 256)).astype(BF16)
        spread = jnp.where(lanes_ref[...] == within[None], values[None], jnp.zeros((), BF16))
        spread_ref[:, 256 * c : 256 * (c + 1)] = spread.reshape(256, 256)
        plane = jnp.right_shift(targets, 8).astype(F32)
        for i in range(2):
            wide = jnp.broadcast_to(plane[:, 128 * i : 128 * (i + 1)], (128, 128))
            column_ref[pl.ds(16 * c + 8 * i, 8)] = wide.T.astype(BF16).reshape(8, CAP, 128)

    def deposits(p, c, n):
        chunk = w_recv[pl.ds(c * PER, n * PER)]
        column = column_ref[pl.ds(c * PER, n * PER)]
        parts = []
        for i in range(2):
            here = jnp.broadcast_to(lax.convert_element_type(2 * p + i, F32), (CAP, 128))
            part = jnp.where(column == here.astype(BF16)[None], chunk, jnp.zeros((), BF16))
            parts.append(part.reshape(n * 256, 128))
        added = jnp.dot(
            spread_ref[:, 256 * c : 256 * (c + n)],
            jnp.concatenate(parts, axis=1),
            preferred_element_type=F32,
        )
        return added[:, :128], added[:, 128:]

    copies = {}

    def copy(name, src, dst, where):
        at = len(copies)
        copies[name] = pltpu.make_async_remote_copy(
            src_ref=src,
            dst_ref=dst,
            send_sem=hsend.at[at],
            recv_sem=hrecv.at[at],
            device_id=neighbour(*where),
            device_id_type=MESH,
        )

    sides = ((-1, 0, 1), (1, VX - R, 0))
    ends = ((0, -1), (1, 1))
    for dx, start, slot in sides:
        copy(("x", dx), u_ref.at[pl.ds(start, R)], xrecv.at[pl.ds(slot * R, R)], (dx, 0, 0))
        copy(("zx", dx), zrecv.at[start // R], zxrecv.at[slot], (dx, 0, 0))
    copy(("z",), zsend, zrecv, (0, 0, 1))
    for d, dy in ends:
        copy(("y", dy), ysend.at[d], yrecv.at[d], (0, dy, 0))
        copy(("zy", dy), esend.at[d], erecv.at[d, pl.ds(0, 4)], (0, dy, 1))
        for dx, start, slot in sides:
            copy(
                ("xy", dx, dy),
                ysend.at[d, pl.ds(start // 2, 4)],
                yxrecv.at[d, pl.ds(slot * 4, 4)],
                (dx, dy, 0),
            )
            copy(("zxy", dx, dy), esend.at[d, start // R], erecv.at[d, 4 + slot], (dx, dy, 1))

    last = len(BATCHES) - 1
    for group, (c, n) in enumerate(BATCHES):
        first = max(1, c * PER)
        count = (c + n) * PER - first
        wait_bytes(meta_r.at[pl.ds(first, count)], mrecv.at[group])
        for i in range(n):
            prepare(c + i)
        wait_bytes(w_recv.at[pl.ds(first, count)], wrecv.at[group])
        if group == last:
            break

        def deposit(p, carry, group=group, c=c, n=n):
            for i, mine in enumerate(deposits(p, c, n)):
                if group == 0:
                    acc[2 * p + i] = mine
                else:
                    acc[2 * p + i] += mine
            return carry

        lax.fori_loop(0, VX // 2, deposit, 0, unroll=4)

    load_blocks = pltpu.make_async_copy(blk_v, blk_s, bsem.at[0])
    load_blocks.start()
    load_design.wait()

    edge = jnp.where(gz == 0, VZ - R, 0)
    zi, zl = iota((128, 128), 0), iota((128, 128), 1)
    pick = jnp.where(zi == edge + jnp.bitwise_and(zl, 7), 1.0, 0.0).astype(BF16)
    eighth = jnp.right_shift(zl, 3)

    def update(p, carry):
        pieces = []
        n = lax.div(p, 4)
        packed = packs[n]
        for i, mine in enumerate(deposits(p, *BATCHES[last])):
            x = 2 * p + i
            moved = jnp.clip(design[x] - 0.5 * (acc[x] + mine), 0.0, 1.0) - 0.5
            pieces.append(moved)
            moved = moved.astype(BF16)
            u_ref[x] = moved
            edges = jnp.dot(moved, pick, preferred_element_type=F32)
            j = 2 * lax.rem(p, 4) + i
            packed = jnp.where(eighth == j, edges[:128], packed)
            packed = jnp.where(eighth == R + j, edges[128:], packed)
        packs[n] = packed
        ysend[0, p] = jnp.concatenate([m[:R] for m in pieces], axis=0).astype(BF16)
        ysend[1, p] = jnp.concatenate([m[VY - R :] for m in pieces], axis=0).astype(BF16)
        return carry

    lax.fori_loop(0, VX // 2, update, 0, unroll=4)
    for n in range(VX // R):
        packed = packs[n]
        zsend[n] = packed.astype(BF16)
        esend[0, n] = packed[:R]
        esend[1, n] = packed[128 - R :]
    for kind in ("z", "zy", "y", "zxy", "xy", "x"):
        for name in copies:
            if name[0] == kind:
                copies[name].start()

    halo_at = jnp.where(gz == 0, VZ, -R) + jnp.bitwise_and(zi, 7)
    kernel_z = jnp.concatenate([cone(zi - zl), cone(halo_at - zl)], axis=0)
    kernel_z = kernel_z.astype(F32).astype(BF16)
    global_z = gz * VZ + iota((1, 128), 1)
    total = jnp.zeros((1, 128), I32)
    for m in range(-R, R + 1):
        at = global_z + m
        total = total + jnp.where(jnp.logical_and(at >= 0, at < 2 * VZ), R + 1 - abs(m), 0)
    scale_z = 1.0 / total.astype(F32)
    lane_group = jnp.right_shift(iota((16, 128), 1), 3)
    group_b = lane_group.astype(F32).astype(BF16)
    half_row = iota((16, 128), 0) < R

    def smooth_z(plane, halo, j):
        tiles = halo.reshape(8, 16, 128)
        kept = [
            jnp.where(group_b[None] == h, tiles, jnp.zeros((), BF16)).reshape(128, 128)
            for h in (j, R + j)
        ]
        both = jnp.concatenate([plane, jnp.concatenate(kept, axis=0)], axis=1)
        return (jnp.dot(both, kernel_z, preferred_element_type=F32) * scale_z).astype(BF16)

    def smooth_rows(rows, edges):
        kept = []
        for part, j in edges:
            tile = jnp.concatenate([part, part], axis=0)
            wanted = jnp.where(half_row, j, j + 1)
            kept.append(jnp.where(lane_group == wanted, tile, 0.0).astype(BF16))
        both = jnp.concatenate(
            [rows.reshape(16 * len(edges), 128), jnp.concatenate(kept, axis=0)], axis=1
        )
        both = jnp.dot(both, kernel_z, preferred_element_type=F32) * scale_z
        return both.astype(BF16).reshape(len(edges), 16, 128)

    band_y = cone(iota((VY, VY), 0) - iota((VY, VY), 1)).astype(F32).astype(BF16)
    oi, ki = iota((32, 32), 0), iota((32, 32), 1)
    same = jnp.right_shift(oi, 3) == jnp.right_shift(ki, 3)
    o8, k8 = jnp.bitwise_and(oi, 7), jnp.bitwise_and(ki, 7)
    below = cone(o8 - (k8 - R))
    above = cone((R + k8) - o8)
    rim_y = jnp.where(same, jnp.where(oi < 16, below, above), 0).astype(F32).astype(BF16)
    scale = 1.0 / ((R + 1) * (R + 1))

    def smooth_y(za, zb, low, high):
        smooth = jnp.dot(band_y, jnp.concatenate([za, zb], axis=1), preferred_element_type=F32)
        rims = jnp.concatenate([low, high], axis=0)
        extra = jnp.dot(rim_y, rims, preferred_element_type=F32)
        out = []
        for i in range(2):
            mine = smooth[:, 128 * i : 128 * (i + 1)]
            top = mine[:R] + extra[R * i : R * (i + 1)]
            end = mine[VY - R :] + extra[16 + R * i : 16 + R * (i + 1)]
            out.append(jnp.concatenate([top, mine[R : VY - R], end], axis=0) * scale)
        return out

    copies[("z",)].wait_recv()
    for dx, start, slot in sides:
        copies[("zx", dx)].start()
    for x in range(VX):
        z_ref[x] = smooth_z(u_ref[x], zrecv[x // R], x % R)
    rows = []
    for d, dy in ends:
        copies[("y", dy)].wait_recv()
        copies[("zy", dy)].wait_recv()
        edges = [(erecv[d, q // 4], R * d + 2 * (q % 4)) for q in range(VX // 2)]
        rows.append(smooth_rows(yrecv[d], edges))
    for q in range(VX // 2):
        pair = smooth_y(z_ref[2 * q], z_ref[2 * q + 1], rows[1][q], rows[0][q])
        y_ref[2 * q], y_ref[2 * q + 1] = pair

    top = math.tanh(4.0)
    strip_rows = 32

    def project(begin, end):
        def strip(s, carry):
            span = pl.ds(pl.multiple_of(s * strip_rows, strip_rows), strip_rows)

            def at(i):
                if i < 0:
                    return rim_ref[i + R, span, :]
                if i >= VX:
                    return rim_ref[i - VX + R, span, :]
                return y_ref[i, span, :]

            total = (R + 1) * at(begin)
            slope = at(begin + R + 1) - at(begin)
            for m in range(1, R + 1):
                low, high = at(begin - m), at(begin + m)
                total = total + (R + 1 - m) * (high + low)
                slope = slope + (high - low)
            for o in range(begin, end):
                proj[o, span, :] = 0.5 + (0.5 / top) * jnp.tanh((8.0 * scale) * total)
                if o < end - 1:
                    total = total + slope
                    if o < end - 2:
                        slope = slope + (at(o + R + 2) - 2.0 * at(o + 1) + at(o - R))
            return carry

        lax.fori_loop(0, VY // strip_rows, strip, 0)
        span = pl.ds(begin, end - begin)
        pltpu.make_async_copy(proj.at[span], out_hbm.at[span], osem.at[0]).start()

    project(R, VX - R)

    for dx, start, slot in sides:
        copies[("x", dx)].wait_recv()
        copies[("zx", dx)].wait_recv()
    for i in range(2 * R):
        zx_ref[i] = smooth_z(xrecv[i], zxrecv[i // R], i % R)
    rows = []
    for d, dy in ends:
        for dx, start, slot in sides:
            copies[("xy", dx, dy)].wait_recv()
            copies[("zxy", dx, dy)].wait_recv()
        edges = [(erecv[d, 4 + q // 4], R * d + 2 * (q % 4)) for q in range(R)]
        rows.append(smooth_rows(yxrecv[d], edges))
    for q in range(R):
        pair = smooth_y(zx_ref[2 * q], zx_ref[2 * q + 1], rows[1][q], rows[0][q])
        rim_ref[2 * q], rim_ref[2 * q + 1] = pair
    project(0, R)
    project(VX - R, VX)

    load_blocks.wait()
    flat = proj.reshape(VX * VY, VZ)
    ones = jnp.ones((8, 128), BF16)
    lanes = (((1,), (1,)), ((), ()))

    def ratio_row(r):
        for j in range(128):
            row = jnp.bitwise_and(blk_s[r, j], VX * VY - 1)
            picked[pl.ds(j, 1), :] = flat[pl.ds(row, 1), :]
        w = w_recv[pl.ds(r * 8, 8)].reshape(128, 128)
        product = w.astype(F32) * picked[...]
        high = product.astype(BF16)
        low = (product - high.astype(F32)).astype(BF16)
        over = lax.dot_general(ones, high, lanes, preferred_element_type=F32)
        over = over + lax.dot_general(ones, low, lanes, preferred_element_type=F32)
        under = lax.dot_general(ones, w, lanes, preferred_element_type=F32)
        ratios[r] = (over / under)[:1]

    def give_back(r, first):
        for i in range(first, 8):
            pltpu.make_async_remote_copy(
                src_ref=ratios.at[r],
                dst_ref=returned.at[me],
                send_sem=rsend.at[0],
                recv_sem=rrecv.at[0],
                device_id=tile_device(lax.rem(me + TILES - 8 * r - i, TILES)),
                device_id_type=MESH,
            ).start()

    ratio_row(0)
    give_back(0, 1)
    returned[me] = ratios[0]

    def row_step(r, carry):
        ratio_row(r)
        give_back(r, 0)
        return carry

    lax.fori_loop(1, TILES // 8, row_step, 0)

    offset = jnp.bitwise_and(iota((128, TILES), 1) + (TILES - me), 7)
    chosen = jnp.right_shift(iota((128, TILES), 0), 4) == offset
    live = live_mask(counts_ref[...])
    wait_bytes(returned.at[pl.ds(1, TILES - 1)], rrecv.at[0])
    ratio = jnp.where(chosen, returned[:, 0, :].T, 0.0)
    ratio = jnp.sum(ratio.reshape(8, CAP, TILES), axis=0)
    ratio = jnp.where(live, ratio, 0.0)
    high = ratio.astype(BF16)
    low = (ratio - high.astype(F32)).astype(BF16)
    left = []
    for part in (high, low):
        part = part.astype(F32)
        rows = [jnp.broadcast_to(part[r : r + 1], (16, 128)) for r in range(CAP)]
        left.append(jnp.concatenate(rows, axis=1) * high_ref[...])
    left = jnp.concatenate(left, axis=0).astype(BF16)
    total = lax.dot_general(left, low_ref[...], lanes, preferred_element_type=F32)
    density_ref[...] = total[:16] + total[16:]

    for name in copies:
        copies[name].wait_send()
    wait_bytes(meta_s.at[pl.ds(1, TILES - 1)], msend.at[0])
    wait_bytes(w_recv.at[pl.ds(1, TILES - 1)], wsend.at[0])
    wait_bytes(returned.at[pl.ds(1, TILES - 1)], rsend.at[0])
    wait_bytes(proj, osem.at[0])


def hand_over(in_hbm, out_hbm, held, load_sem, store_sem):
    loads, stores = [], []
    for i in range(PIECES):
        span = pl.ds(i * (VX // PIECES), VX // PIECES)
        loads.append(pltpu.make_async_copy(in_hbm.at[span], held.at[span], load_sem.at[i]))
        stores.append(pltpu.make_async_copy(held.at[span], out_hbm.at[span], store_sem.at[i]))
    for load in loads:
        load.start()
    for load, store in zip(loads, stores):
        load.wait()
        store.start()
    for store in stores:
        store.wait()


VMEM = pl.BlockSpec(memory_space=pltpu.VMEM)
SMEM = pl.BlockSpec(memory_space=pltpu.SMEM)
ANY = pl.BlockSpec(memory_space=pl.ANY)
DMA = pltpu.SemaphoreType.DMA
LIMIT = 60 << 20


def body(
    design,
    forward_edges,
    adjoint_edges,
    edge_basis,
    quad_weights,
    slot_weights,
    slot_elements,
    slot_blocks,
    slot_counts,
):
    shape = jax.ShapeDtypeStruct
    projected, density = pl.pallas_call(
        step_kernel,
        name="density_step",
        out_shape=(shape((VX, VY, VZ), F32), shape((16, 128), F32)),
        in_specs=[ANY, VMEM, VMEM, VMEM, SMEM, VMEM, VMEM, VMEM, VMEM],
        out_specs=(ANY, VMEM),
        scratch_shapes=[
            pltpu.VMEM((VX, VY, VZ), F32),
            pltpu.VMEM((VX, VY, VZ), F32),
            pltpu.VMEM((VX, VY, VZ), BF16),
            pltpu.VMEM((VX, VY, VZ), BF16),
            pltpu.VMEM((2 * R, VY, VZ), BF16),
            pltpu.VMEM((2 * R, VY, VZ), BF16),
            pltpu.VMEM((VX, VY, VZ), F32),
            pltpu.VMEM((2 * R, VY, VZ), F32),
            pltpu.VMEM((VX, VY, VZ), F32),
            pltpu.VMEM((128, 128), F32),
            pltpu.VMEM((TILES, CAP, 128), BF16),
            pltpu.VMEM((TILES, 1, 128), F32),
            pltpu.VMEM((TILES, 1, 128), F32),
            pltpu.VMEM((16, 16, 256), BF16),
            pltpu.VMEM((VY, TILES * CAP), BF16),
            pltpu.VMEM((TILES, CAP, 128), BF16),
            pltpu.VMEM((16, 128), I32),
            pltpu.SMEM((16, 128), I32),
            pltpu.VMEM((TILES // 8, 1, 128), F32),
            pltpu.VMEM((TILES, 1, 128), F32),
            pltpu.VMEM((2, 16, 16, 128), BF16),
            pltpu.VMEM((2, 16, 16, 128), BF16),
            pltpu.VMEM((2, 8, 16, 128), BF16),
            pltpu.VMEM((4, 128, 128), F32),
            pltpu.VMEM((16, TILES * CAP), F32),
            pltpu.VMEM((128, TILES * CAP), BF16),
            pltpu.VMEM((4, 128, 128), BF16),
            pltpu.VMEM((4, 128, 128), BF16),
            pltpu.VMEM((2, 128, 128), BF16),
            pltpu.VMEM((2, 4, R, 128), F32),
            pltpu.VMEM((2, 6, R, 128), F32),
            DMA((1,)),
            DMA((1,)),
            DMA((len(BATCHES),)),
            DMA((1,)),
            DMA((len(BATCHES),)),
            DMA((17,)),
            DMA((17,)),
            DMA((1,)),
            DMA((1,)),
            DMA((1,)),
            DMA((1,)),
        ],
        compiler_params=pltpu.CompilerParams(
            collective_id=1, has_side_effects=True, vmem_limit_bytes=LIMIT
        ),
    )(
        design,
        forward_edges.transpose(1, 0, 2),
        adjoint_edges.transpose(1, 0, 2),
        edge_basis.T,
        quad_weights,
        slot_weights,
        slot_elements.T,
        slot_blocks.T,
        slot_counts,
    )
    projected = pl.pallas_call(
        hand_over,
        name="hand_over",
        out_shape=shape((VX, VY, VZ), F32),
        in_specs=[ANY],
        out_specs=ANY,
        scratch_shapes=[pltpu.VMEM((VX, VY, VZ), F32), DMA((PIECES,)), DMA((PIECES,))],
    )(projected)
    return projected, density.reshape(-1)


def solution(mesh):
    in_specs = (
        P("tx", "ty", "gz"),
        P(None, None, ("tx", "ty", "gz")),
        P(None, None, ("tx", "ty", "gz")),
        P(),
        P(),
        P(("tx", "ty", "gz"), None, None),
        P(("tx", "ty", "gz"), None),
        P(("tx", "ty", "gz"), None),
        P(("tx", "ty", "gz"), None),
    )
    out_specs = (P("tx", "ty", "gz"), P(("tx", "ty", "gz")))
    return jax.shard_map(body, mesh=mesh, in_specs=in_specs, out_specs=out_specs, check_vma=False)
```

time: 261 us -> 77.5 us (0.30)
  other arithmetic: 106 us -> 0 us
  Pallas kernels: 0 us -> 76.1 us
  waiting for transfers between devices: 60.6 us -> 0 us
  starting transfers between devices: 48.2 us -> 0 us
  local copies, waits for them, and re-layouts: 41.1 us -> 0.61 us
  matrix products: 3.91 us -> 0 us
    pallas_call x0 -> x2, Pallas kernels: none -> 76.1 us  [the longest x1 72.5 us: body(): pl.pallas_call(step_kernel, name='density_step', out_shape=(shape((VX, VY...]
    div x2 -> x0, other arithmetic: 54.6 us -> none  [the longest x1 54.6 us: project(): (math.tanh(sharp * middle) + jnp.tanh(sharp * (filtered - middle))) / spa...]
    all_to_all x3 -> x0, waiting for transfers between devices: 40.6 us -> none  [the longest x1 30 us: sent_together(): lax.all_to_all(both, axis, split_axis=split_dim, concat_axis=concat_dim,...]
    all_to_all x3 -> x0, starting transfers between devices: 37 us -> none  [the longest x1 14.9 us: body(): lax.all_to_all(slot_blocks, ('tx', 'ty'), split_axis=0, concat_axis=0, ti...]
    scatter-add x2 -> x0, other arithmetic: 25.6 us -> none  [the longest x1 13.7 us: body(): gradient_blocks.at[arrived_blocks.reshape(-1)]]
    ppermute x6 -> x0, waiting for transfers between devices: 20 us -> none  [the longest x3 17.2 us: extended(): lax.ppermute(lax.slice_in_dim(block, block.shape[dim] - width, None, axis...]
    gather x4 -> x0, local copies, waits for them, and re-layouts: 19.4 us -> none  [the longest x3 11.8 us: body(): sensitivities[slot_elements]]
    add x3 -> x0, other arithmetic: 17 us -> none  [along(): summed + kernel[offset] * lax.slice_in_dim(padded, offset, offset + lengt...]
  transfers between devices with their start and end apart: 9 -> 0, of which waited for: 6 -> 0; matrix products, arithmetic and copies ran while one was open for 9% -> 0% of each run, Pallas kernels for 0% -> 0%
where the time goes in v2:
time: 77.5 us; the launch traced here: 77.3 us
  Pallas kernels  76.1 us (98%)
    pallas_call x1, Pallas kernels, body(): pl.pallas_call(step_kernel, name='density_step', out_shape=(shape((VX, VY...  72.5 us
    pallas_call x1, Pallas kernels, body(): pl.pallas_call(hand_over, name='hand_over', out_shape=shape((VX, VY, VZ),...  3.58 us

profile of v2, /device:TPU:1, one launch (start us, length us, event | category | flops | bytes accessed | tf_op | source)
XLA Modules:
  0.0 77.3 jit_solution(17056179613851104577)
XLA Ops:
  0.6 72.5 %density_step.1 = (f32[32,256,128]{2,1,0:T(8,128)}, f32[16,128]{1,0:T(8,128)}) custom-call(f32[32,256,128]{2,1,0:T(8,128)} %design_hbm.1, f32[12,2,2048]{2,1,0:T(2,128)} %bitcast.6, f32[12,2,2048]{2,1,0:T(2,128)} %bitcast.7, f32[12,24]{1,0:T(8,128)} %bitcast.8, f32[8]{0:T(128)} %quad_ref.1, bf16[128,16,128]{2,1,0:T(8,128)(2,1)} %weights_ref.1, ...), custom_call_target="tpu_custom_call" | custom-call | tf_op jit(solution)/shard_map/density_step/pallas_call | solution.py:542
  73.1 0.0 copy-start
  73.1 3.6 %hand_over.1 = f32[32,256,128]{2,1,0:T(8,128)} custom-call(f32[32,256,128]{2,1,0:T(8,128)} %get-tuple-element.4.in_hbm), custom_call_target="tpu_custom_call" | custom-call | tf_op jit(solution)/shard_map/hand_over/pallas_call | solution.py:606
  76.7 0.0 copy-done
  76.7 0.6 copy.12
Async XLA Ops:
  73.1 3.6 %copy-start = (f32[16,128]{1,0:T(8,128)S(1)}, f32[16,128]{1,0:T(8,128)}, u32[]{:S(2)}) copy-start(f32[16,128]{1,0:T(8,128)} %get-tuple-element.5) | copy-start | bytes 24580

commit v3 on v2

--- a/solution.py
+++ b/solution.py
@@ -200,7 +200,8 @@
     def prepare(c):
         va, ta = slots(2 * c)
         vb, tb = slots(2 * c + 1)
-        values = jnp.broadcast_to(jnp.concatenate([va, vb], axis=1), (16, 256)).astype(BF16)
+        values = -0.5 * jnp.concatenate([va, vb], axis=1)
+        values = jnp.broadcast_to(values, (16, 256)).astype(BF16)
         targets = jnp.concatenate([ta, tb], axis=1)
         within = jnp.bitwise_and(targets, 255).astype(F32)
         within = jnp.broadcast_to(within, (16, 256)).astype(BF16)
@@ -257,6 +258,7 @@
             )
             copy(("zxy", dx, dy), esend.at[d, start // R], erecv.at[d, 4 + slot], (dx, dy, 1))
 
+    load_design.wait()
     last = len(BATCHES) - 1
     for group, (c, n) in enumerate(BATCHES):
         first = max(1, c * PER)
@@ -271,7 +273,7 @@
         def deposit(p, carry, group=group, c=c, n=n):
             for i, mine in enumerate(deposits(p, c, n)):
                 if group == 0:
-                    acc[2 * p + i] = mine
+                    acc[2 * p + i] = design[2 * p + i] + mine
                 else:
                     acc[2 * p + i] += mine
             return carry
@@ -280,7 +282,6 @@
 
     load_blocks = pltpu.make_async_copy(blk_v, blk_s, bsem.at[0])
     load_blocks.start()
-    load_design.wait()
 
     edge = jnp.where(gz == 0, VZ - R, 0)
     zi, zl = iota((128, 128), 0), iota((128, 128), 1)
@@ -293,7 +294,7 @@
         packed = packs[n]
         for i, mine in enumerate(deposits(p, *BATCHES[last])):
             x = 2 * p + i
-            moved = jnp.clip(design[x] - 0.5 * (acc[x] + mine), 0.0, 1.0) - 0.5
+            moved = jnp.clip(acc[x] + mine, 0.0, 1.0) - 0.5
             pieces.append(moved)
             moved = moved.astype(BF16)
             u_ref[x] = moved
@@ -444,12 +445,16 @@
     ones = jnp.ones((8, 128), BF16)
     lanes = (((1,), (1,)), ((), ()))
 
-    def ratio_row(r):
+    def gather(r):
+        base = pl.multiple_of(128 * lax.rem(r, 2), 128)
         for j in range(128):
             row = jnp.bitwise_and(blk_s[r, j], VX * VY - 1)
-            picked[pl.ds(j, 1), :] = flat[pl.ds(row, 1), :]
+            picked[pl.ds(base + j, 1), :] = flat[pl.ds(row, 1), :]
+
+    def ratio_row(r):
+        base = pl.multiple_of(128 * lax.rem(r, 2), 128)
         w = w_recv[pl.ds(r * 8, 8)].reshape(128, 128)
-        product = w.astype(F32) * picked[...]
+        product = w.astype(F32) * picked[pl.ds(base, 128), :]
         high = product.astype(BF16)
         low = (product - high.astype(F32)).astype(BF16)
         over = lax.dot_general(ones, high, lanes, preferred_element_type=F32)
@@ -468,16 +473,24 @@
                 device_id_type=MESH,
             ).start()
 
-    ratio_row(0)
-    give_back(0, 1)
+    def row_step(r, carry):
+        give_back(r - 2, 0)
+        ratio_row(r - 1)
+        gather(r)
+        return carry
+
+    rows = TILES // 8
+    gather(jnp.int32(0))
+    ratio_row(jnp.int32(0))
+    gather(jnp.int32(1))
+    give_back(jnp.int32(0), 1)
     returned[me] = ratios[0]
-
-    def row_step(r, carry):
-        ratio_row(r)
-        give_back(r, 0)
-        return carry
-
-    lax.fori_loop(1, TILES // 8, row_step, 0)
+    ratio_row(jnp.int32(1))
+    gather(jnp.int32(2))
+    lax.fori_loop(3, rows, row_step, 0)
+    ratio_row(jnp.int32(rows - 1))
+    give_back(jnp.int32(rows - 2), 0)
+    give_back(jnp.int32(rows - 1), 0)
 
     offset = jnp.bitwise_and(iota((128, TILES), 1) + (TILES - me), 7)
     chosen = jnp.right_shift(iota((128, TILES), 0), 4) == offset
@@ -555,7 +568,7 @@
             pltpu.VMEM((VX, VY, VZ), F32),
             pltpu.VMEM((2 * R, VY, VZ), F32),
             pltpu.VMEM((VX, VY, VZ), F32),
-            pltpu.VMEM((128, 128), F32),
+            pltpu.VMEM((256, 128), F32),
             pltpu.VMEM((TILES, CAP, 128), BF16),
             pltpu.VMEM((TILES, 1, 128), F32),
             pltpu.VMEM((TILES, 1, 128), F32),

time: 77.5 us -> 76.4 us (0.986)
  Pallas kernels: 76.1 us -> 75 us
    pallas_call x1, Pallas kernels: 72.5 us -> 71.4 us  [body(): pl.pallas_call(step_kernel, name='density_step', out_shape=(shape((VX, VY...]
where the time goes in v3:
time: 76.4 us; the launch traced here: 76.3 us
  Pallas kernels  75 us (98%)
    pallas_call x1, Pallas kernels, body(): pl.pallas_call(step_kernel, name='density_step', out_shape=(shape((VX, VY...  71.4 us
    pallas_call x1, Pallas kernels, body(): pl.pallas_call(hand_over, name='hand_over', out_shape=shape((VX, VY, VZ),...  3.58 us

profile of v3, /device:TPU:1, one launch (start us, length us, event | category | flops | bytes accessed | tf_op | source)
XLA Modules:
  0.0 76.3 jit_solution(8329625239683029917)
XLA Ops:
  0.6 71.4 %density_step.1 = (f32[32,256,128]{2,1,0:T(8,128)}, f32[16,128]{1,0:T(8,128)}) custom-call(f32[32,256,128]{2,1,0:T(8,128)} %design_hbm.1, f32[12,2,2048]{2,1,0:T(2,128)} %bitcast.6, f32[12,2,2048]{2,1,0:T(2,128)} %bitcast.7, f32[12,24]{1,0:T(8,128)} %bitcast.8, f32[8]{0:T(128)} %quad_ref.1, bf16[128,16,128]{2,1,0:T(8,128)(2,1)} %weights_ref.1, ...), custom_call_target="tpu_custom_call" | custom-call | tf_op jit(solution)/shard_map/density_step/pallas_call | solution.py:555
  72.1 0.0 copy-start
  72.1 3.6 %hand_over.1 = f32[32,256,128]{2,1,0:T(8,128)} custom-call(f32[32,256,128]{2,1,0:T(8,128)} %get-tuple-element.4.in_hbm), custom_call_target="tpu_custom_call" | custom-call | tf_op jit(solution)/shard_map/hand_over/pallas_call | solution.py:619
  75.7 0.0 copy-done
  75.7 0.6 copy.12
Async XLA Ops:
  72.1 3.6 %copy-start = (f32[16,128]{1,0:T(8,128)S(1)}, f32[16,128]{1,0:T(8,128)}, u32[]{:S(2)}) copy-start(f32[16,128]{1,0:T(8,128)} %get-tuple-element.5) | copy-start | bytes 24580

commit v4 on v3

--- a/solution.py
+++ b/solution.py
@@ -15,7 +15,7 @@
 R = 8
 PER = 16
 PIECES = 8
-BATCHES = ((0, 4), (4, 2), (6, 2))
+BATCHES = ((0, 4), (4, 2), (6, 1), (7, 1))
 F32, BF16, I32 = jnp.float32, jnp.bfloat16, jnp.int32
 HIGHEST = lax.Precision.HIGHEST
 

time: 76.4 us -> 76.1 us (level)
  no operation moved by 1% of the time
where the time goes in v4:
time: 76.1 us; the launch traced here: 76 us
  Pallas kernels  74.7 us (98%)
    pallas_call x1, Pallas kernels, body(): pl.pallas_call(step_kernel, name='density_step', out_shape=(shape((VX, VY...  71.1 us
    pallas_call x1, Pallas kernels, body(): pl.pallas_call(hand_over, name='hand_over', out_shape=shape((VX, VY, VZ),...  3.58 us

profile of v4, /device:TPU:1, one launch (start us, length us, event | category | flops | bytes accessed | tf_op | source)
XLA Modules:
  0.0 76.0 jit_solution(5527210523104000873)
XLA Ops:
  0.6 71.1 %density_step.1 = (f32[32,256,128]{2,1,0:T(8,128)}, f32[16,128]{1,0:T(8,128)}) custom-call(f32[32,256,128]{2,1,0:T(8,128)} %design_hbm.1, f32[12,2,2048]{2,1,0:T(2,128)} %bitcast.6, f32[12,2,2048]{2,1,0:T(2,128)} %bitcast.7, f32[12,24]{1,0:T(8,128)} %bitcast.8, f32[8]{0:T(128)} %quad_ref.1, bf16[128,16,128]{2,1,0:T(8,128)(2,1)} %weights_ref.1, ...), custom_call_target="tpu_custom_call" | custom-call | tf_op jit(solution)/shard_map/density_step/pallas_call | solution.py:555
  71.8 0.0 copy-start
  71.8 3.6 %hand_over.1 = f32[32,256,128]{2,1,0:T(8,128)} custom-call(f32[32,256,128]{2,1,0:T(8,128)} %get-tuple-element.4.in_hbm), custom_call_target="tpu_custom_call" | custom-call | tf_op jit(solution)/shard_map/hand_over/pallas_call | solution.py:619
  75.4 0.0 copy-done
  75.4 0.6 copy.12
Async XLA Ops:
  71.8 3.6 %copy-start = (f32[16,128]{1,0:T(8,128)S(1)}, f32[16,128]{1,0:T(8,128)}, u32[]{:S(2)}) copy-start(f32[16,128]{1,0:T(8,128)} %get-tuple-element.5) | copy-start | bytes 24580
